TPU v7x, 256 devices: a whole 4x4x8 slice. The times are simulated.
256 devices in a mesh: dp: 8 (over z_hi, x), space: 32 (over z_lo, y, core).
Axes of the slice: x: 4, y: 4, z: 8 (z_hi: 2, z_lo: 4; z = z_hi * 4 + z_lo), core: 2. Of those that a mesh axis runs over, the one named last changes fastest.
Arguments:
- crop: bfloat16 [8, 4, 128, 64, 64], P('dp', None, 'space'), may hold values from -6 to 6
- filter_one: bfloat16 [3, 3, 3, 4, 32], replicated, may hold values from -0.625 to 0.625
- filter_two: bfloat16 [3, 3, 3, 32, 64], replicated, may hold values from -0.21875 to 0.21875
- cotangent: bfloat16 [8, 64, 32, 16, 16], P('dp', None, 'space'), may hold values from -1 to 1
Outputs:
- features: bfloat16 [8, 64, 32, 16, 16], P('dp', None, 'space')
- grad_one: float32 [3, 3, 3, 4, 32], replicated
- grad_two: float32 [3, 3, 3, 32, 64], replicated
All inputs are finite; a program needn't handle non-finite values.
Results may differ from a plain program's by a relative error of at most 0.0045.
The roundings to bfloat16 on the way count: a program that leaves them out, or rounds other values in their place, can miss the bound.
Values may be sent and summed in bfloat16 or wider, within the bound.
A program may use at most 128 MiB of HBM per device.

v0:
```python
import jax
import jax.numpy as jnp
from jax import lax
from jax.sharding import PartitionSpec as P


def with_halo(shard, sides, width):
    for axis, dim in sides:
        count, length = (lax.axis_size(axis), shard.shape[dim])
        up = [(i, (i + 1) % count) for i in range(count - 1)]
        down = [(j, i) for i, j in up]
        last = lax.slice_in_dim(shard, length - width, length, axis=dim)
        leading = lax.slice_in_dim(shard, 0, width, axis=dim)
        before = lax.ppermute(last, axis, up)
        after = lax.ppermute(leading, axis, down)
        shard = jnp.concatenate([before, shard, after], axis=dim)
    return shard


def leaky(value):
    return jnp.where(value > 0, value, 0.3 * value)


def slope(value):
    return jnp.where(value > 0, 1.0, 0.3)


def pooled(value):
    shape = value.shape
    blocks = value.reshape(shape[0], shape[1], shape[2] // 2, 2, shape[3] // 2, 2, shape[4] // 2, 2)
    return blocks.mean(axis=(3, 5, 7))


def widened(value):
    shape = value.shape
    spread = jnp.broadcast_to(
        value[:, :, :, None, :, None, :, None],
        (shape[0], shape[1], shape[2], 2, shape[3], 2, shape[4], 2),
    )
    return spread.reshape(shape[0], shape[1], 2 * shape[2], 2 * shape[3], 2 * shape[4])


def convolve(source, kernel):
    return lax.conv_general_dilated(
        source,
        kernel,
        (1, 1, 1),
        ((0, 0), (1, 1), (1, 1)),
        dimension_numbers=("NCDHW", "DHWIO", "NCDHW"),
        preferred_element_type=jnp.float32,
    )


def flipped(kernel):
    return jnp.transpose(kernel[::-1, ::-1, ::-1], (0, 1, 2, 4, 3))


def filter_grad(source, gradient):
    planes, extent_y, extent_z = (gradient.shape[2], gradient.shape[3], gradient.shape[4])
    padded = jnp.pad(source, ((0, 0), (0, 0), (0, 0), (1, 1), (1, 1)))
    partials = []
    for offset in range(27):
        shift_a, shift_b, shift_c = (offset // 9, offset // 3 % 3, offset % 3)
        window = padded[
            :,
            :,
            shift_a : shift_a + planes,
            shift_b : shift_b + extent_y,
            shift_c : shift_c + extent_z,
        ]
        partials.append(
            jnp.einsum("bcxyz,bdxyz->cd", window, gradient, preferred_element_type=jnp.float32)
        )
    return jnp.stack(partials).reshape(3, 3, 3, source.shape[1], gradient.shape[1])


def local(crop, filter_one, filter_two, cotangent):
    crop_wide = with_halo(crop, (("space", 2),), 1)
    z_one = convolve(crop_wide, filter_one)
    maps_one = pooled(leaky(z_one)).astype(jnp.bfloat16)
    maps_wide = with_halo(maps_one, (("space", 2),), 1)
    z_two = convolve(maps_wide, filter_two)
    grad_pre_two = (slope(z_two) * widened(cotangent.astype(jnp.float32)) * 0.125).astype(
        jnp.bfloat16
    )
    grad_outer = with_halo(grad_pre_two, (("space", 2),), 1)
    features = pooled(leaky(z_two)).astype(jnp.bfloat16)
    local_two = filter_grad(maps_wide, grad_pre_two)
    back_one = convolve(grad_outer, flipped(filter_two))
    grad_pre_one = (slope(z_one) * widened(back_one) * 0.125).astype(jnp.bfloat16)
    local_one = filter_grad(crop_wide, grad_pre_one)
    grad_one, grad_two = lax.psum((local_one, local_two), ("dp", "space"))
    return (features, grad_one, grad_two)


def solution(mesh):
    placed = (P("dp", None, "space", None, None), P(), P(), P("dp", None, "space", None, None))
    return jax.shard_map(
        local,
        mesh=mesh,
        in_specs=placed,
        out_specs=(P("dp", None, "space", None, None), P(), P()),
        check_vma=False,
    )
```

profile of v0, /device:TPU:1, one launch (start us, length us, event | category | flops | bytes accessed | tf_op | source)
XLA Modules:
  0.0 399.3 jit_solution(16076839817375526808)
XLA Ops:
  8.5 4.6 %collective-permute-start = (bf16[1,4,1,64,64]{4,1,3,2,0:T(4,128)(2,1)S(1)}, bf16[1,4,1,64,64]{4,1,3,2,0:T(4,128)(2,1)S(1)}, u32[]{:S(2)}, u32[]{:S(2)}) collective-permute-start(bf16[1,4,1,64,64]{4,1,3,2,0:T(4,128)(2,1)S(1)} %get-tuple-element.20), channel_id=1, source_target_pairs={{0,1},{1,2},{2,3},{3,4},{4,5},{5,6},{6,7},{7,8},{8,9},{9,10},{10,1... | collective-permute-start | bytes 98312 | tf_op jit(solution)/shard_map/ppermute | solution.py:14
  19.8 3.7 copy.327
  25.2 24.3 %compare_select_fusion = (f32[4,64,8,9,32]{4,2,3,1,0:T(8,128)}, f32[4,64,8,9,32]{4,2,3,1,0:T(8,128)}) fusion(pred[8,9]{0,1:T(8,128)(4,1)S(1)} %copy-done.15, bf16[3,3,3,4,32]{4,3,2,1,0:T(4,128)(2,1)S(1)} %copy-done.14, bf16[4,6,64,1,7,2]{4,0,5,2,1,3:T(4,128)(2,1)S(1)} %slice.254, bf16[4,6,64,1,8,9]{4,0,5,2,1,3:T(4,128)(2,1)} %copy.327), kind=kOutput, calls=%fused_computation.1 | convolution fusion | flops 129835008 | bytes 4989768 | tf_op jit(solution)/shard_map/conv_general_dilated | solution.py:44
  49.5 8.7 %copy.328 = f32[4,64,8,9,32]{1,4,3,2,0:T(8,128)} copy(f32[4,64,8,9,32]{4,2,3,1,0:T(8,128)} %get-tuple-element.10) | data formatting | bytes 4718592 | tf_op jit(solution)/shard_map/jit(_where)/select_n | solution.py:21
  58.2 4.6 %slice_bitcast_fusion.1 = f32[1,32,4,64,64]{3,1,4,2,0:T(8,128)} fusion(f32[4,64,1,72,32]{1,4,3,0,2:T(8,128)} %bitcast.701), kind=kLoop, calls=%fused_computation.14 | loop fusion | bytes 4194304 | tf_op jit(solution)/shard_map/jit(_where)/select_n | solution.py:21
  62.8 9.3 %copy.329 = f32[1,32,4,64,64]{1,4,3,2,0:T(8,128)} copy(f32[1,32,4,64,64]{3,1,4,2,0:T(8,128)} %slice_bitcast_fusion.1) | data formatting | bytes 4194304 | tf_op jit(solution)/shard_map/jit(_where)/select_n | solution.py:21
  72.1 9.1 %reduce_sum.21 = f32[32,2,32,32]{0,3,2,1:T(8,128)S(1)} reduce(f32[32,2,2,32,2,32,2]{0,6,5,4,3,2,1:T(2,128)} %bitcast.698, f32[]{:T(128)} %constant.5.clone.1), dimensions={2,4,6}, to_apply=%region_0.1 | reduce | flops 458752 | bytes 2359300 | tf_op jit(solution)/shard_map/reduce_sum | solution.py:31
  84.4 2.4 collective-permute-start.3
  88.4 8.7 %copy.335 = f32[4,64,8,9,32]{1,4,3,2,0:T(8,128)} copy(f32[4,64,8,9,32]{4,2,3,1,0:T(8,128)} %get-tuple-element.9) | data formatting | bytes 4718592 | tf_op jit(solution)/shard_map/jit(_where)/select_n | solution.py:25
  97.8 2.3 pad_maximum_fusion
  100.1 3.8 copy.455
  103.9 2.6 pad.12.clone
  106.5 3.0 copy.333
  110.7 4.6 %compare_select_fusion.1 = (f32[2,32,8,5,64]{4,2,3,1,0:T(8,128)S(1)}, f32[2,32,8,5,64]{4,2,3,1,0:T(8,128)}) fusion(bf16[3,3,3,32,64]{4,3,2,1,0:T(8,128)(2,1)S(1)} %copy-done, bf16[32,4,32,1,7,2]{0,4,5,2,1,3:T(8,128)(2,1)S(1)} %slice.258, bf16[32,4,32,1,8,5]{0,4,5,2,1,3:T(8,128)(2,1)} %copy.333, pred[8,5]{0,1:T(8,128)(4,1)S(1)} %copy-done.16), kind=kOutput, calls=%fused_computation.34 | convolution fusion | flops 279412736 | bytes 1863720 | tf_op jit(solution)/shard_map/conv_general_dilated | solution.py:44
  136.9 3.1 collective-permute-start.4
  140.0 2.1 collective-permute-start.5
  144.9 2.8 collective-permute-done.5
  148.9 5.1 %fusion.32 = f32[2,32,8,5,32]{4,2,3,1,0:T(8,128)S(1)} fusion(bf16[3,3,3,32,64]{4,3,2,1,0:T(8,128)(2,1)S(1)} %copy-done, bf16[64,4,32,1,7,2]{0,4,5,2,1,3:T(8,128)(2,1)S(1)} %slice.264, bf16[64,4,32,1,8,5]{0,4,5,2,1,3:T(8,128)(2,1)S(1)} %copy.339, pred[8,5]{0,1:T(8,128)(4,1)S(1)} %copy-done.16), kind=kOutput, calls=%fused_computation.36 | convolution fusion | flops 280051712 | bytes 1323048 | tf_op jit(solution)/shard_map/conv_general_dilated | solution.py:44
  155.0 7.6 %broadcast_in_dim.44 = f32[32,2,2,32,2,32,2]{0,6,5,4,3,2,1:T(2,128)} broadcast(f32[32,2,32,32]{0,3,2,1:T(8,128)S(1)} %copy.341), dimensions={0,1,3,5} | broadcast | bytes 2359296 | tf_op jit(solution)/shard_map/broadcast_in_dim | solution.py:36
  162.6 7.8 %copy.342 = f32[1,32,4,64,64]{3,1,4,2,0:T(8,128)} copy(f32[1,32,4,64,64]{1,4,3,2,0:T(8,128)} %bitcast.699) | data formatting | bytes 4194304 | tf_op jit(solution)/shard_map/broadcast_in_dim | solution.py:36
  170.4 5.8 %fusion.14 = bf16[32,4,64,64]{2,0,3,1:T(8,128)(2,1)} fusion(f32[1,32,4,64,64]{3,1,4,2,0:T(8,128)} %copy.342, f32[4,64,1,72,32]{1,4,3,0,2:T(8,128)} %bitcast.700), kind=kLoop, calls=%fused_computation.20 | loop fusion | flops 1572864 | bytes 5242880 | tf_op jit(solution)/shard_map/reshape.3
  176.3 5.7 %copy.343 = bf16[32,4,64,64]{3,0,2,1:T(8,128)(2,1)S(1)} copy(bf16[32,4,64,64]{2,0,3,1:T(8,128)(2,1)} %fusion.14) | data formatting | bytes 2097152 | tf_op jit(solution)/shard_map/reshape.3
  201.1 85.7 %psum.14 = f32[3,3,3,4,32]{4,3,2,1,0:T(4,128)} all-reduce(f32[3,3,3,4,32]{4,3,2,1,0:T(4,128)S(1)} %bitcast.714), channel_id=1, replica_groups=mesh['dp'=8,'space'=32] {'dp','space'}, use_global_device_ids=true, to_apply=%region_3.4 | all-reduce | flops 3456 | bytes 27648 | tf_op jit(solution)/shard_map/psum | solution.py:92
  286.8 103.6 %all-reduce.4.cloned.1.call-done = f32[3,3,3,32,64]{4,3,2,1,0:T(8,128)} async-done(((f32[3,3,3,32,64]{4,3,2,1,0:T(8,128)}), f32[3,3,3,32,64]{4,3,2,1,0:T(8,128)}) %all-reduce.4.cloned.1.call-update) | async-done | bytes 221200 | tf_op jit(solution)/shard_map/psum | solution.py:92
  (130 shorter events, 63.3 us)
Async XLA Ops:
  7.2 103.6 %copy-start = (bf16[3,3,3,32,64]{4,3,2,1,0:T(8,128)(2,1)S(1)}, bf16[3,3,3,32,64]{4,3,2,1,0:T(8,128)(2,1)}, u32[]{:S(2)}) copy-start(bf16[3,3,3,32,64]{4,3,2,1,0:T(8,128)(2,1)} %param.6) | copy-start | bytes 331780
  7.2 383.2 %all-reduce.4.cloned.1.call-start = ((), (), s32[]{:S(2)}) async-start(), calls=%async_computation | async-start | bytes 884736 | tf_op jit(solution)/shard_map/psum | solution.py:92
  8.5 6.5 %collective-permute-start = (bf16[1,4,1,64,64]{4,1,3,2,0:T(4,128)(2,1)S(1)}, bf16[1,4,1,64,64]{4,1,3,2,0:T(4,128)(2,1)S(1)}, u32[]{:S(2)}, u32[]{:S(2)}) collective-permute-start(bf16[1,4,1,64,64]{4,1,3,2,0:T(4,128)(2,1)S(1)} %get-tuple-element.20), channel_id=1, source_target_pairs={{0,1},{1,2},{2,3},{3,4},{4,5},{5,6},{6,7},{7,8},{8,9},{9,10},{10,1... | collective-permute-start | bytes 98312 | tf_op jit(solution)/shard_map/ppermute | solution.py:14
  13.1 5.6 %collective-permute-start.1 = (bf16[1,4,1,64,64]{4,1,3,2,0:T(4,128)(2,1)S(1)}, bf16[1,4,1,64,64]{4,1,3,2,0:T(4,128)(2,1)S(1)}, u32[]{:S(2)}, u32[]{:S(2)}) collective-permute-start(bf16[1,4,1,64,64]{4,1,3,2,0:T(4,128)(2,1)S(1)} %get-tuple-element.19), channel_id=1, source_target_pairs={{1,0},{2,1},{3,2},{4,3},{5,4},{6,5},{7,6},{8,7},{9,8},{10,9},{11,1... | collective-permute-start | bytes 98312 | tf_op jit(solution)/shard_map/ppermute | solution.py:15
  15.0 0.6 copy-start.10
  18.7 0.6 copy-start.8
  19.8 5.4 %copy-start.14 = (bf16[3,3,3,4,32]{4,3,2,1,0:T(4,128)(2,1)S(1)}, bf16[3,3,3,4,32]{4,3,2,1,0:T(4,128)(2,1)}, u32[]{:S(2)}) copy-start(bf16[3,3,3,4,32]{4,3,2,1,0:T(4,128)(2,1)} %param.5) | copy-start | bytes 20740
  19.8 5.4 %copy-start.15 = (pred[8,9]{0,1:T(8,128)(4,1)S(1)}, pred[8,9]{0,1:T(8,128)(4,1)}, u32[]{:S(2)}) copy-start(pred[8,9]{0,1:T(8,128)(4,1)} %constant.39) | copy-start | bytes 220
  81.6 5.2 %copy-start.13 = (bf16[1,64,1,16,16]{1,4,3,2,0:T(8,128)(2,1)S(1)}, bf16[1,64,1,16,16]{1,4,3,2,0:T(8,128)(2,1)}, u32[]{:S(2)}) copy-start(bf16[1,64,1,16,16]{1,4,3,2,0:T(8,128)(2,1)} %param.7) | copy-start | bytes 98308
  81.6 5.9 %copy-start.3 = (bf16[1,4,4,64,64]{4,3,2,1,0:T(8,128)(2,1)S(1)}, bf16[1,4,4,64,64]{4,3,2,1,0:T(8,128)(2,1)}, u32[]{:S(2)}) copy-start(bf16[1,4,4,64,64]{4,3,2,1,0:T(8,128)(2,1)} %param.4) | copy-start | bytes 393220
  82.5 14.6 %collective-permute-start.2 = (bf16[1,32,1,32,32]{4,1,3,2,0:T(8,128)(2,1)}, bf16[1,32,1,32,32]{4,1,3,2,0:T(8,128)(2,1)S(1)}, u32[]{:S(2)}, u32[]{:S(2)}) collective-permute-start(bf16[1,32,1,32,32]{4,1,3,2,0:T(8,128)(2,1)} %get-tuple-element.17), channel_id=1, source_target_pairs={{0,1},{1,2},{2,3},{3,4},{4,5},{5,6},{6,7},{7,8},{8,9},{9,10},{10,1... | collective-permute-start | bytes 196616 | tf_op jit(solution)/shard_map/ppermute | solution.py:14
  84.4 13.4 %collective-permute-start.3 = (bf16[1,32,1,32,32]{4,1,3,2,0:T(8,128)(2,1)S(1)}, bf16[1,32,1,32,32]{4,1,3,2,0:T(8,128)(2,1)}, u32[]{:S(2)}, u32[]{:S(2)}) collective-permute-start(bf16[1,32,1,32,32]{4,1,3,2,0:T(8,128)(2,1)S(1)} %get-tuple-element.18), channel_id=1, source_target_pairs={{1,0},{2,1},{3,2},{4,3},{5,4},{6,5},{7,6},{8,7},{9,8},{10,9},{11,1... | collective-permute-start | bytes 196616 | tf_op jit(solution)/shard_map/ppermute | solution.py:15
  97.1 0.7 copy-start.6
  106.5 4.2 %copy-start.16 = (pred[8,5]{0,1:T(8,128)(4,1)S(1)}, pred[8,5]{0,1:T(8,128)(4,1)}, u32[]{:S(2)}) copy-start(pred[8,5]{0,1:T(8,128)(4,1)} %constant.38) | copy-start | bytes 124
  115.4 0.9 copy-start.4
  118.3 1.9 copy-start.7
  134.8 2.0 copy-start.2
  136.0 0.8 copy-start.5
  136.9 8.1 %collective-permute-start.4 = (bf16[1,64,1,32,32]{1,3,4,2,0:T(8,128)(2,1)S(1)}, bf16[1,64,1,32,32]{1,3,4,2,0:T(8,128)(2,1)S(1)}, u32[]{:S(2)}, u32[]{:S(2)}) collective-permute-start(bf16[1,64,1,32,32]{1,3,4,2,0:T(8,128)(2,1)S(1)} %get-tuple-element.15), channel_id=1, source_target_pairs={{0,1},{1,2},{2,3},{3,4},{4,5},{5,6},{6,7},{7,8},{8,9},{9,10},{10,1... | collective-permute-start | bytes 393224 | tf_op jit(solution)/shard_map/ppermute | solution.py:14
  140.0 7.7 %collective-permute-start.5 = (bf16[1,64,1,32,32]{1,3,4,2,0:T(8,128)(2,1)S(1)}, bf16[1,64,1,32,32]{1,3,4,2,0:T(8,128)(2,1)S(1)}, u32[]{:S(2)}, u32[]{:S(2)}) collective-permute-start(bf16[1,64,1,32,32]{1,3,4,2,0:T(8,128)(2,1)S(1)} %get-tuple-element.16), channel_id=1, source_target_pairs={{1,0},{2,1},{3,2},{4,3},{5,4},{6,5},{7,6},{8,7},{9,8},{10,9},{11,1... | collective-permute-start | bytes 393224 | tf_op jit(solution)/shard_map/ppermute | solution.py:15
  183.3 1.5 copy-start.11
  189.6 1.6 copy-start.1
  189.6 1.6 copy-start.12
  196.1 1.5 copy-start.9
Sparse Core Ops, SparseCore 0:
  136.9 253.4 all-reduce.3
where the time goes:
time: 407 us; the launch traced here: 399 us
  waiting for transfers between devices  108 us (27%)
  blocking collectives  85.7 us (21%)
  local copies, waits for them, and re-layouts  83.9 us (21%)
  matrix products  71.1 us (17%)
  other arithmetic  19.3 us (5%)
  starting transfers between devices  16.1 us (4%)
  between operations  14.9 us (4%)
    psum x1, waiting for transfers between devices, local(): grad_one, grad_two = lax.psum((local_one, local_two), ('dp', 'space'))  104 us
    psum x1, blocking collectives, local(): grad_one, grad_two = lax.psum((local_one, local_two), ('dp', 'space'))  85.7 us
    dot_general x54, matrix products, filter_grad(): jnp.einsum('bcxyz,bdxyz->cd', window, gradient, preferred_element_type=jn...  37.1 us
    conv_general_dilated x3, matrix products, convolve(): lax.conv_general_dilated(source, kernel, (1, 1, 1), ((0, 0), (1, 1), (1,...  34 us
    select_n x4, local copies, waits for them, and re-layouts, leaky(): return jnp.where(value > 0, value, 0.3 * value)  24.2 us
    broadcast_in_dim x6, local copies, waits for them, and re-layouts, widened(): jnp.broadcast_to(value[:, :, :, None, :, None, :, None], (shape[0], shape...  17.1 us
    unnamed x41, local copies, waits for them, and re-layouts  12.5 us
    conv_general_dilated x7, local copies, waits for them, and re-layouts, convolve(): lax.conv_general_dilated(source, kernel, (1, 1, 1), ((0, 0), (1, 1), (1,...  10.5 us
  transfers between devices with their start and end apart: 7, of which 3 were waited for; matrix products, arithmetic and copies ran while one was open for 17% of the time, Pallas kernels for 0%

commit v1 on v0

--- a/solution.py
+++ b/solution.py
@@ -89,7 +89,9 @@
     back_one = convolve(grad_outer, flipped(filter_two))
     grad_pre_one = (slope(z_one) * widened(back_one) * 0.125).astype(jnp.bfloat16)
     local_one = filter_grad(crop_wide, grad_pre_one)
-    grad_one, grad_two = lax.psum((local_one, local_two), ("dp", "space"))
+    grad_one, grad_two = lax.psum(
+        lax.psum((local_one, local_two), axis_name="space"), axis_name="dp"
+    )
     return (features, grad_one, grad_two)
 
 

time: 407 us -> 616 us (1.51)
  the two profiles are of different devices: /device:TPU:1 before, /device:TPU:0 now
where the time goes in v1:
time: 616 us; the launch traced here: 609 us
  waiting for transfers between devices  214 us (35%)
  blocking collectives  192 us (31%)
  local copies, waits for them, and re-layouts  83.9 us (14%)
  matrix products  71.1 us (12%)
  other arithmetic  19.3 us (3%)
  between operations  14.9 us (2%)
  starting transfers between devices  13.3 us (2%)
    psum x1, waiting for transfers between devices, local(): lax.psum((local_one, local_two), axis_name='space')  214 us
    psum x1, blocking collectives, local(): lax.psum((local_one, local_two), axis_name='space')  138 us
    psum x1, blocking collectives, local(): lax.psum(lax.psum((local_one, local_two), axis_name='space'), axis_name='...  53.9 us
    dot_general x54, matrix products, filter_grad(): jnp.einsum('bcxyz,bdxyz->cd', window, gradient, preferred_element_type=jn...  37.1 us
    conv_general_dilated x3, matrix products, convolve(): lax.conv_general_dilated(source, kernel, (1, 1, 1), ((0, 0), (1, 1), (1,...  34 us
    select_n x4, local copies, waits for them, and re-layouts, leaky(): return jnp.where(value > 0, value, 0.3 * value)  24.2 us
    broadcast_in_dim x6, local copies, waits for them, and re-layouts, widened(): jnp.broadcast_to(value[:, :, :, None, :, None, :, None], (shape[0], shape...  17.1 us
    unnamed x41, local copies, waits for them, and re-layouts  12.5 us
  transfers between devices with their start and end apart: 8, of which 2 were waited for; matrix products, arithmetic and copies ran while one was open for 11% of the time, Pallas kernels for 0%

profile of v1, /device:TPU:0, one launch (start us, length us, event | category | flops | bytes accessed | tf_op | source)
XLA Modules:
  0.0 608.6 jit_solution(12801883025810173174)
XLA Ops:
  14.2 3.7 copy.327
  17.9 1.7 slice.254
  19.6 24.2 %compare_select_fusion = (f32[4,64,8,9,32]{4,2,3,1,0:T(8,128)}, f32[4,64,8,9,32]{4,2,3,1,0:T(8,128)}) fusion(pred[8,9]{0,1:T(8,128)(4,1)S(1)} %copy-done.15, bf16[3,3,3,4,32]{4,3,2,1,0:T(4,128)(2,1)S(1)} %copy-done.14, bf16[4,6,64,1,7,2]{4,0,5,2,1,3:T(4,128)(2,1)S(1)} %slice.254, bf16[4,6,64,1,8,9]{4,0,5,2,1,3:T(4,128)(2,1)} %copy.327), kind=kOutput, calls=%fused_computation.1 | convolution fusion | flops 129835008 | bytes 4989768 | tf_op jit(solution)/shard_map/conv_general_dilated | solution.py:44
  43.8 8.7 %copy.328 = f32[4,64,8,9,32]{1,4,3,2,0:T(8,128)} copy(f32[4,64,8,9,32]{4,2,3,1,0:T(8,128)} %get-tuple-element.10) | data formatting | bytes 4718592 | tf_op jit(solution)/shard_map/jit(_where)/select_n | solution.py:21
  52.5 4.6 slice_bitcast_fusion.1
  57.1 9.3 %copy.329 = f32[1,32,4,64,64]{1,4,3,2,0:T(8,128)} copy(f32[1,32,4,64,64]{3,1,4,2,0:T(8,128)} %slice_bitcast_fusion.1) | data formatting | bytes 4194304 | tf_op jit(solution)/shard_map/jit(_where)/select_n | solution.py:21
  66.4 9.1 %reduce_sum.21 = f32[32,2,32,32]{0,3,2,1:T(8,128)S(1)} reduce(f32[32,2,2,32,2,32,2]{0,6,5,4,3,2,1:T(2,128)} %bitcast.698, f32[]{:T(128)} %constant.5.clone.1), dimensions={2,4,6}, to_apply=%region_0.1 | reduce | flops 458752 | bytes 2359300 | tf_op jit(solution)/shard_map/reduce_sum | solution.py:31
  76.7 4.8 collective-permute-start.2
  84.5 8.7 %copy.335 = f32[4,64,8,9,32]{1,4,3,2,0:T(8,128)} copy(f32[4,64,8,9,32]{4,2,3,1,0:T(8,128)} %get-tuple-element.9) | data formatting | bytes 4718592 | tf_op jit(solution)/shard_map/jit(_where)/select_n | solution.py:25
  93.9 2.3 pad_maximum_fusion
  96.2 3.8 copy.455
  100.0 2.6 pad.12.clone
  102.6 3.0 copy.333
  106.8 4.6 compare_select_fusion.1
  132.9 3.0 collective-permute-start.4
  141.5 5.1 fusion.32
  147.5 7.6 %broadcast_in_dim.44 = f32[32,2,2,32,2,32,2]{0,6,5,4,3,2,1:T(2,128)} broadcast(f32[32,2,32,32]{0,3,2,1:T(8,128)S(1)} %copy.341), dimensions={0,1,3,5} | broadcast | bytes 2359296 | tf_op jit(solution)/shard_map/broadcast_in_dim | solution.py:36
  155.1 7.8 %copy.342 = f32[1,32,4,64,64]{3,1,4,2,0:T(8,128)} copy(f32[1,32,4,64,64]{1,4,3,2,0:T(8,128)} %bitcast.699) | data formatting | bytes 4194304 | tf_op jit(solution)/shard_map/broadcast_in_dim | solution.py:36
  163.0 5.8 fusion.14
  168.8 5.7 copy.343
  192.9 214.0 %all-reduce.5.cloned.1.call-done = f32[3,3,3,32,64]{4,3,2,1,0:T(8,128)} async-done(((f32[3,3,3,32,64]{4,3,2,1,0:T(8,128)}), f32[3,3,3,32,64]{4,3,2,1,0:T(8,128)}) %all-reduce.5.cloned.1.call-update) | async-done | bytes 221200 | tf_op jit(solution)/shard_map/psum | solution.py:93
  407.7 138.2 %psum.28 = f32[3,3,3,4,32]{4,3,2,1,0:T(4,128)S(1)} all-reduce(f32[3,3,3,4,32]{4,3,2,1,0:T(4,128)S(1)} %bitcast.714), channel_id=1, replica_groups=mesh['dp'=8,'space'=32] {'space'}, use_global_device_ids=true, to_apply=%region_3.4 | all-reduce | flops 3456 | bytes 27648 | tf_op jit(solution)/shard_map/psum | solution.py:93
  545.8 53.9 %psum.29 = f32[3,3,3,4,32]{4,3,2,1,0:T(4,128)} all-reduce(f32[3,3,3,4,32]{4,3,2,1,0:T(4,128)S(1)} %psum.28), channel_id=1, replica_groups=mesh['dp'=8,'space'=32] {'dp'}, use_global_device_ids=true, to_apply=%region_4.5 | all-reduce | flops 3456 | bytes 27648 | tf_op jit(solution)/shard_map/psum | solution.py:92
  599.8 1.8 copy.567
  (134 shorter events, 59.6 us)
Async XLA Ops:
  7.2 99.6 %copy-start = (bf16[3,3,3,32,64]{4,3,2,1,0:T(8,128)(2,1)S(1)}, bf16[3,3,3,32,64]{4,3,2,1,0:T(8,128)(2,1)}, u32[]{:S(2)}) copy-start(bf16[3,3,3,32,64]{4,3,2,1,0:T(8,128)(2,1)} %param.6) | copy-start | bytes 331780
  7.2 399.7 %all-reduce.5.cloned.1.call-start = ((), (), s32[]{:S(2)}) async-start(), calls=%async_computation | async-start | bytes 884736 | tf_op jit(solution)/shard_map/psum | solution.py:93
  8.5 2.6 collective-permute-start
  9.8 3.2 collective-permute-start.1
  11.1 0.6 copy-start.10
  14.1 5.4 copy-start.14
  14.1 5.4 copy-start.15
  75.8 7.0 %copy-start.13 = (bf16[1,64,1,16,16]{1,4,3,2,0:T(8,128)(2,1)S(1)}, bf16[1,64,1,16,16]{1,4,3,2,0:T(8,128)(2,1)}, u32[]{:S(2)}) copy-start(bf16[1,64,1,16,16]{1,4,3,2,0:T(8,128)(2,1)} %param.7) | copy-start | bytes 98308
  75.9 7.7 %copy-start.3 = (bf16[1,4,4,64,64]{4,3,2,1,0:T(8,128)(2,1)S(1)}, bf16[1,4,4,64,64]{4,3,2,1,0:T(8,128)(2,1)}, u32[]{:S(2)}) copy-start(bf16[1,4,4,64,64]{4,3,2,1,0:T(8,128)(2,1)} %param.4) | copy-start | bytes 393220
  76.7 16.4 %collective-permute-start.2 = (bf16[1,32,1,32,32]{4,1,3,2,0:T(8,128)(2,1)}, bf16[1,32,1,32,32]{4,1,3,2,0:T(8,128)(2,1)S(1)}, u32[]{:S(2)}, u32[]{:S(2)}) collective-permute-start(bf16[1,32,1,32,32]{4,1,3,2,0:T(8,128)(2,1)} %get-tuple-element.17), channel_id=1, source_target_pairs={{0,1},{1,2},{2,3},{3,4},{4,5},{5,6},{6,7},{7,8},{8,9},{9,10},{10,1... | collective-permute-start | bytes 196616 | tf_op jit(solution)/shard_map/ppermute | solution.py:14
  81.6 12.3 %collective-permute-start.3 = (bf16[1,32,1,32,32]{4,1,3,2,0:T(8,128)(2,1)S(1)}, bf16[1,32,1,32,32]{4,1,3,2,0:T(8,128)(2,1)}, u32[]{:S(2)}, u32[]{:S(2)}) collective-permute-start(bf16[1,32,1,32,32]{4,1,3,2,0:T(8,128)(2,1)S(1)} %get-tuple-element.18), channel_id=1, source_target_pairs={{1,0},{2,1},{3,2},{4,3},{5,4},{6,5},{7,6},{8,7},{9,8},{10,9},{11,1... | collective-permute-start | bytes 196616 | tf_op jit(solution)/shard_map/ppermute | solution.py:15
  93.2 0.7 copy-start.6
  102.6 4.2 copy-start.16
  111.4 0.9 copy-start.4
  114.4 1.9 copy-start.7
  130.8 2.1 copy-start.2
  132.0 0.8 copy-start.5
  132.8 467.0 %all-reduce.7.cloned.1.call-start = ((), (), s32[]{:S(2)}) async-start(), calls=%async_computation.1 | async-start | bytes 884736 | tf_op jit(solution)/shard_map/psum | solution.py:92
  132.9 7.3 %collective-permute-start.4 = (bf16[1,64,1,32,32]{1,3,4,2,0:T(8,128)(2,1)S(1)}, bf16[1,64,1,32,32]{1,3,4,2,0:T(8,128)(2,1)S(1)}, u32[]{:S(2)}, u32[]{:S(2)}) collective-permute-start(bf16[1,64,1,32,32]{1,3,4,2,0:T(8,128)(2,1)S(1)} %get-tuple-element.15), channel_id=1, source_target_pairs={{0,1},{1,2},{2,3},{3,4},{4,5},{5,6},{6,7},{7,8},{8,9},{9,10},{10,1... | collective-permute-start | bytes 393224 | tf_op jit(solution)/shard_map/ppermute | solution.py:14
  136.0 4.3 collective-permute-start.5
  175.9 1.5 copy-start.11
  182.2 1.6 copy-start.1
  182.2 1.6 copy-start.12
  188.7 1.5 copy-start.9
  (1 other events, 0.6 us)
Sparse Core Ops, SparseCore 0:
  132.9 273.9 all-reduce.4
  409.8 107.0 all-reduce.6
